TPU v7x, 32 devices: a whole 2x2x4 slice. The times are simulated.
32 devices in a mesh: dp: 8 (over z, x), head: 4 (over y, core).
Axes of the slice: x: 2, y: 2, z: 4, core: 2. Of those that a mesh axis runs over, the one named last changes fastest.
Arguments:
- block_input: bfloat16 [16384, 768], P(('dp', 'head')), may hold values from -6 to 6
- norm1_gain: float32 [768], replicated, may hold values from 0.5 to 1.5
- norm1_bias: float32 [768], replicated, may hold values from -0.625 to 0.625
- qkv_weight: bfloat16 [3, 768, 768], P(None, None, 'head'), may hold values from -0.21875 to 0.21875
- qkv_bias: float32 [2, 12, 64], P(None, 'head'), may hold values from -0.625 to 0.625
- proj_weight: bfloat16 [768, 768], P('head'), may hold values from -1.75 to 1.75
- proj_bias: float32 [768], replicated, may hold values from -0.625 to 0.625
- norm2_gain: float32 [768], replicated, may hold values from 0.5 to 1.5
- norm2_bias: float32 [768], replicated, may hold values from -0.625 to 0.625
- router_weight: float32 [768, 8], replicated, may hold values from -0.15625 to 0.15625
- up_weight: bfloat16 [8, 768, 3072], P('dp'), may hold values from -0.21875 to 0.21875
- up_bias: float32 [8, 3072], P('dp'), may hold values from -0.625 to 0.625
- down_weight: bfloat16 [8, 3072, 768], P('dp'), may hold values from -1.25 to 1.25
- down_bias: float32 [8, 768], P('dp'), may hold values from -5 to 5
- routes: int32 [16384, 1], P(('dp', 'head')), may hold values from 0 to 7; in each aligned block of 512 rows (0 to 511, 512 to 1023, ...) at most 128 rows name the same one
- lengths: int32 [8, 4], P('dp'), may hold values from 1 to 1024, 2048 in all within a row
- cotangent: bfloat16 [16384, 768], P(('dp', 'head')), may hold values from -6 to 6
Outputs:
- mixed: bfloat16 [16384, 768], P(('dp', 'head'))
- balance: float32 [32], P(('dp', 'head'))
- input_grad: float32 [16384, 768], P(('dp', 'head'))
- norm1_gain_grad: float32 [768], P(('dp', 'head'))
- norm1_bias_grad: float32 [768], P(('dp', 'head'))
- qkv_weight_grad: float32 [3, 768, 768], P(None, 'dp', 'head')
- qkv_bias_grad: float32 [2, 12, 64], P(None, 'head', 'dp')
- proj_weight_grad: float32 [768, 768], P('head', 'dp')
- proj_bias_grad: float32 [768], P(('dp', 'head'))
- norm2_gain_grad: float32 [768], P(('dp', 'head'))
- norm2_bias_grad: float32 [768], P(('dp', 'head'))
- router_weight_grad: float32 [768, 8], P(('dp', 'head'))
- up_weight_grad: float32 [8, 768, 3072], P('dp', None, 'head')
- up_bias_grad: float32 [8, 3072], P('dp', 'head')
- down_weight_grad: float32 [8, 3072, 768], P('dp', 'head')
- down_bias_grad: float32 [8, 768], P('dp', 'head')
Inputs may be any that keep to these rules, and one draw needn't show every extreme that they name: `routes`: among the rows of one device at most 128 name the same expert. `lengths`: each row sums to 2048, and its largest entry is 1024.
All inputs are finite; a program needn't handle non-finite values.
Results may differ from a plain program's by a relative error of at most 0.017.
Values may be sent and summed in bfloat16 or wider, within the bound.
A program may use at most 192 MiB of HBM per device.

v0:
```python
import functools
import jax
import jax.numpy as jnp
from jax import lax
from jax.experimental import pallas as pl
from jax.experimental.pallas import tpu as pltpu
from jax.sharding import PartitionSpec as P

EPSILON = 1e-05
BAL_COEF = 0.01
HIGHEST = lax.Precision.HIGHEST
NEG_LARGE = -1e30
MESH = pl.DeviceIdType.MESH
F32 = jnp.float32
BF16 = jnp.bfloat16
TILE = 256
VMEM_LIMIT = 60 << 20
UNROLL_A = True
UNROLL_B = False


def flip(index, bits):
    out, bit = index, 1
    while bit <= bits:
        if bits & bit:
            out = out + bit - 2 * bit * lax.rem(lax.div(index, bit), 2)
        bit *= 2
    return out


def remote(src, dst, send_sem, recv_sem, device):
    return pltpu.make_async_remote_copy(
        src_ref=src, dst_ref=dst, send_sem=send_sem, recv_sem=recv_sem, device_id=device, device_id_type=MESH
    )


def dot(left, right, dims=((1,), (0,)), precision=None):
    return lax.dot_general(left, right, (dims, ((), ())), precision=precision, preferred_element_type=F32)


def normalize(values, gain, bias):
    average = jnp.mean(values, axis=-1, keepdims=True)
    centred = values - average
    variance = jnp.mean(centred * centred, axis=-1, keepdims=True)
    inverse = lax.rsqrt(variance + EPSILON)
    scaled = centred * inverse
    return (scaled * gain + bias, scaled, inverse)


def norm_backward(grad_normed, scaled, inverse, gain):
    grad_scaled = grad_normed * gain
    first_mean = jnp.mean(grad_scaled, axis=-1, keepdims=True)
    second_mean = jnp.mean(grad_scaled * scaled, axis=-1, keepdims=True)
    return inverse * (grad_scaled - first_mean - scaled * second_mean)


def slot_layouts(routes, experts, cap):
    rows = routes.shape[1]
    count = max(8, experts)
    expert = lax.broadcasted_iota(jnp.int32, (count, rows), 0)
    hot = (routes == expert).astype(F32)
    upto = lax.broadcasted_iota(jnp.int32, (rows, rows), 0) <= lax.broadcasted_iota(jnp.int32, (rows, rows), 1)
    rank = dot(hot.astype(BF16), upto.astype(F32).astype(BF16))
    slot_row = jnp.sum((rank - 1.0) * hot, axis=0, keepdims=True)
    flat_row = jnp.sum((rank - 1.0 + cap * expert.astype(F32)) * hot, axis=0, keepdims=True)
    return hot, flat_row.astype(jnp.int32), slot_row.astype(jnp.int32)


def barrier_signal(peers):
    barrier = pltpu.get_barrier_semaphore()
    for peer in peers:
        pl.semaphore_signal(barrier, inc=1, device_id=peer, device_id_type=MESH)


def barrier_wait(count):
    pl.semaphore_wait(pltpu.get_barrier_semaphore(), count)


def kernel_a(
    n_dp, x_ref, g1_ref, b1_ref, w_ref, qb_ref, proj_ref, routes_ref, cot_ref, len_ref,
    gath_o, qkv_o, p_o, ctx_o, ctxf_o, projf_o, cots_o,
    gath, qkv, p_st, bias_s, ctx_s, out_s, disp,
    ag_s, ag_r, pj_s, pj_r, cx_s, cx_r, ct_s, ct_r, p_sem, loc,
):
    tok, width = x_ref.shape
    heads = qb_ref.shape[0]
    hd = qb_ref.shape[2]
    group = 4 * tok
    tiles = group // TILE
    reach = group // 2 // TILE + 1
    cap = cots_o.shape[0] // n_dp
    d = lax.axis_index("dp")
    h = lax.axis_index("head")
    barrier_signal([(d, flip(h, k)) for k in (1, 2, 3)] + [(flip(d, r), h) for r in range(1, n_dp)])

    def block(index):
        return pl.ds(pl.multiple_of(index * tok, tok), tok)

    gain, bias = g1_ref[...][None, :], b1_ref[...][None, :]

    def norm_rows(i, carry):
        normed, _, _ = normalize(x_ref[pl.ds(pl.multiple_of(i * 64, 64), 64), :].astype(F32), gain, bias)
        gath[pl.ds(pl.multiple_of(h * tok + i * 64, 64), 64), :] = normed.astype(BF16)
        return carry

    lax.fori_loop(0, tok // 64, norm_rows, 0)
    barrier_wait(3 + n_dp - 1)

    chunks = 4
    step = tok // chunks

    def part(index, i):
        return gath.at[pl.ds(pl.multiple_of(index * tok + i * step, step), step), :]

    sib, cross, diag = flip(h, 1), flip(h, 2), flip(h, 3)
    to_cross = [remote(part(h, i), part(h, i), ag_s.at[i], ag_r.at[i], (d, cross)) for i in range(chunks)]
    to_sib = remote(gath.at[block(h), :], gath.at[block(h), :], ag_s.at[2 * chunks], ag_r.at[2 * chunks], (d, sib))
    onward = [
        remote(part(cross, i), part(cross, i), ag_s.at[chunks + i], ag_r.at[chunks + i], (d, sib)) for i in range(chunks)
    ]
    for copy in to_cross:
        copy.start()
    to_sib.start()
    proj_copies = [
        remote(proj_ref, projf_o.at[h], pj_s.at[k], pj_r.at[k], (d, flip(h, k))) for k in (1, 2, 3)
    ]

    hot_t, flat_row, slot_row = slot_layouts(routes_ref[...], n_dp, cap)
    slot_iota = lax.broadcasted_iota(jnp.int32, (cap, tok), 0)

    def dispatch(e, carry):
        hot = (flat_row == slot_iota + e * cap).astype(F32).astype(BF16)
        disp[pl.ds(pl.multiple_of(e * cap, cap), cap), :] = dot(hot, cot_ref[...]).astype(BF16)
        return carry

    lax.fori_loop(0, n_dp, dispatch, 0)

    def slots(index):
        return pl.ds(pl.multiple_of(index * cap, cap), cap)

    cot_copies = [
        remote(disp.at[slots(flip(d, r)), :], cots_o.at[pl.ds(r * cap, cap), :], ct_s.at[r], ct_r.at[r], (flip(d, r), h))
        for r in range(1, n_dp)
    ]
    for copy in cot_copies:
        copy.start()
    cot_own = pltpu.make_async_copy(disp.at[slots(d), :], cots_o.at[pl.ds(0, cap), :], ct_s.at[0])
    cot_own.start()

    def project(index):
        def rows_of(i, carry):
            at = pl.ds(pl.multiple_of(index * tok + i * TILE, TILE), TILE)
            rows = gath[at, :]
            for c in range(3):
                out = dot(rows, w_ref[c], ((1,), (1,)))
                for a in range(heads):
                    piece = out[:, a * hd : (a + 1) * hd]
                    if c != 1:
                        piece = piece + qb_ref[a, c // 2 : c // 2 + 1, :]
                    piece = piece.astype(BF16)
                    if c == 0:
                        piece = piece * jnp.asarray(hd ** (-0.5), BF16)
                    qkv[c, a, at, :] = piece
            return carry

        lax.fori_loop(0, tok // TILE, rows_of, 0)

    project(h)
    to_sib.wait_recv()
    project(sib)
    for i in range(chunks):
        to_cross[i].wait_recv()
        onward[i].start()
    for copy in proj_copies:
        copy.start()
    proj_own = pltpu.make_async_copy(proj_ref, projf_o.at[h], loc.at[0])
    proj_own.start()
    project(cross)
    for i in range(chunks):
        onward[i].wait_recv()
    project(diag)
    gath_copy = pltpu.make_async_copy(gath, gath_o, loc.at[1])
    gath_copy.start()
    qkv_copy = pltpu.make_async_copy(qkv, qkv_o, loc.at[2])
    qkv_copy.start()

    ends = [len_ref[0, 0]]
    for i in range(1, len_ref.shape[1] - 1):
        ends.append(ends[-1] + len_ref[0, i])

    per_block = tok // TILE
    size_t = TILE * 3 // 2
    low_tiles = reach - 1

    def p_copy(t, a, size):
        return pltpu.make_async_copy(p_st.at[a, :, pl.ds(0, size)], p_o.at[a, t, :, pl.ds(0, size)], p_sem.at[a])

    def ctx_rows(t):
        return pl.ds(pl.multiple_of(lax.rem(t, per_block) * size_t, size_t), size_t)

    def ctx_send(t):
        owner = lax.div(t, per_block)
        return remote(ctx_s.at[t], ctxf_o.at[h, ctx_rows(t), :], cx_s.at[t], cx_r.at[h, lax.rem(t, per_block)], (d, owner))

    def ctx_keep(t):
        return pltpu.make_async_copy(ctx_s.at[t], ctxf_o.at[h, ctx_rows(t), :], cx_s.at[t])

    def tile_step(t, size, before, unrolled):
        first = (t + 1) * TILE - size
        rows = pl.ds(pl.multiple_of(t * TILE, TILE), TILE)
        win = pl.ds(pl.multiple_of(first, TILE), size)
        row = t * TILE + lax.broadcasted_iota(jnp.int32, (TILE, 1), 0)
        start = jnp.zeros((TILE, 1), jnp.int32)
        for end in ends:
            start = jnp.where(row >= end, end, start)
        col = first + lax.broadcasted_iota(jnp.int32, (TILE, size), 1)
        bias_s[:, :size] = jnp.where((col >= start) & (col <= row), 0.0, NEG_LARGE)

        def attend(a, carry):
            s = dot(qkv[0, a, rows, :], qkv[1, a, win, :], ((1,), (1,))) + bias_s[:, :size]
            top = jnp.max(s, axis=1, keepdims=True)
            e = jnp.exp(s - top)
            total = jnp.sum(e, axis=1, keepdims=True)
            p = (e * (1.0 / total)).astype(BF16)
            if before:
                p_copy(t, a, before).wait()
            p_st[a, :, :size] = p
            p_copy(t, a, size).start()
            out_s[a] = dot(p, qkv[2, a, win, :])
            return carry

        if unrolled:
            for a in range(heads):
                attend(a, 0)
        else:
            lax.fori_loop(0, heads, attend, 0)
        ctx_s[t] = pack([out_s[a] for a in range(heads)]).astype(BF16)

        @pl.when(h != lax.div(t, per_block))
        def _():
            ctx_send(t).start()

        @pl.when(h == lax.div(t, per_block))
        def _():
            ctx_keep(t).start()

    before = 0
    for t in range(low_tiles):
        tile_step(t, (t + 1) * TILE, before, False)
        before = (t + 1) * TILE
    span = reach * TILE
    p_st[:, :, before:] = jnp.zeros((heads, TILE, span - before), BF16)
    for a in range(heads):
        p_copy(low_tiles - 1, a, before).wait()
        p_copy(low_tiles - 1, a, span).start()

    def high_tile(t, carry):
        tile_step(t, span, span, UNROLL_A)
        return carry

    lax.fori_loop(low_tiles, tiles, high_tile, 0)
    ctx_copy = pltpu.make_async_copy(ctx_s, ctx_o, loc.at[3])
    ctx_copy.start()
    for a in range(heads):
        p_copy(tiles - 1, a, span).wait()

    def sent(t, carry):
        @pl.when(h != lax.div(t, per_block))
        def _():
            ctx_send(t).wait_send()

        @pl.when(h == lax.div(t, per_block))
        def _():
            ctx_keep(t).wait()

        return carry

    lax.fori_loop(0, tiles, sent, 0)
    for k in (1, 2, 3):
        peer = flip(h, k)
        for sub in range(per_block):
            remote(
                ctx_s.at[0], ctxf_o.at[peer, pl.ds(sub * (TILE * 3 // 2), TILE * 3 // 2), :], cx_s.at[0], cx_r.at[peer, sub], (d, peer)
            ).wait_recv()
    for copy in to_cross:
        copy.wait_send()
    to_sib.wait_send()
    for copy in onward:
        copy.wait_send()
    for k in (1, 2, 3):
        proj_copies[k - 1].wait_send()
        peer = flip(h, k)
        remote(proj_ref, projf_o.at[peer], pj_s.at[k], pj_r.at[k], (d, peer)).wait_recv()
    for copy in cot_copies:
        copy.wait()
    for copy in (cot_own, proj_own, gath_copy, qkv_copy, ctx_copy):
        copy.wait()


VM = pl.BlockSpec(memory_space=pltpu.VMEM)
SM = pl.BlockSpec(memory_space=pltpu.SMEM)
ANY = pl.BlockSpec(memory_space=pl.ANY)
DMA = pltpu.SemaphoreType.DMA


def stage_a(n_dp, x, g1, b1, w, qb, proj, routes, cot, lengths, cap):
    tok, width = x.shape
    heads, hd = qb.shape[1:]
    w, qb, routes = w.transpose(0, 2, 1), qb.transpose(1, 0, 2), routes.T
    group = 4 * tok
    tiles = group // TILE
    span = (group // 2 // TILE + 1) * TILE
    cols = heads * hd
    sds = jax.ShapeDtypeStruct
    return pl.pallas_call(
        functools.partial(kernel_a, n_dp),
        out_shape=(
            sds((group, width), BF16),
            sds((3, heads, group, hd), BF16),
            sds((heads, tiles, TILE, span), BF16),
            sds((tiles, TILE * 3 // 2, 128), BF16),
            sds((4, tok * 3 // 2, 128), BF16),
            sds((4, cols, width), BF16),
            sds((n_dp * cap, width), BF16),
        ),
        in_specs=[VM] * 8 + [SM],
        out_specs=(ANY,) * 7,
        scratch_shapes=[
            pltpu.VMEM((group, width), BF16),
            pltpu.VMEM((3, heads, group, hd), BF16),
            pltpu.VMEM((heads, TILE, span), BF16),
            pltpu.VMEM((TILE, span), F32),
            pltpu.VMEM((tiles, TILE * 3 // 2, 128), BF16),
            pltpu.VMEM((heads, TILE, hd), F32),
            pltpu.VMEM((n_dp * cap, width), BF16),
            DMA((9,)), DMA((9,)), DMA((4,)), DMA((4,)), DMA((tiles,)), DMA((4, tok // TILE)),
            DMA((n_dp,)), DMA((n_dp,)), DMA((heads,)), DMA((4,)),
        ],
        compiler_params=pltpu.CompilerParams(collective_id=0, has_side_effects=True, vmem_limit_bytes=VMEM_LIMIT),
    )(x, g1, b1, w, qb, proj, routes, cot, lengths)


def far_first(n_dp):
    half = n_dp // 2
    return list(range(half, n_dp)) + [r for r in range(2, half)] + [1]


def gelu_parts(u):
    return 0.5 * lax.erf(u * 0.7071067811865476) + 0.5, jnp.exp(u * u * -0.5) * 0.3989422804014327


def split3(value):
    high = value.astype(BF16)
    rest = value - high.astype(F32)
    middle = rest.astype(BF16)
    return high, middle, (rest - middle.astype(F32)).astype(BF16)


def fold3(stacked):
    count = stacked.shape[0] // 3
    return stacked[:count] + stacked[count : 2 * count] + stacked[2 * count :]


def differ(index, other, count):
    out, bit = 0, 1
    while bit < count:
        one, two = lax.rem(lax.div(index, bit), 2), lax.rem(lax.div(other, bit), 2)
        out = out + bit * (one + two - 2 * one * two)
        bit *= 2
    return out


def row_to_col(row):
    return jnp.broadcast_to(row, (128, row.shape[1])).T[:, :1]


def col_to_rows(col):
    return jnp.broadcast_to(col, (col.shape[0], 128)).T[:8]


def kernel_m(
    n_dp, x_ref, ctxf, projf, pb_ref, g2_ref, b2_ref, rt_ref, routes_ref, cot_ref, cots, up_h, upb_ref, down_h, downb_ref,
    res, gate_o, prod_o, gres_o, gctx_o, upc_o, upo_o, dno_o, dnr_o, sm_o, bg_o, bal_o,
    stat, nhigh, nlow, low_s, gates_s, left_s, fcol, disp, gsend, rows, rowst, grecv, up, down, ghu, hid, gg, gacc, gin, ggs, ginr, ggr, dsend, dacc, drecv, urecv,
    ld, ra_s, ra_r, ga_s, ga_r, rb_s, rb_r, gb_s, gb_r, ds_s, ds_r, us_s, us_r, out_sem,
):
    tok, width = x_ref.shape
    ff = up.shape[1]
    slots = rows.shape[0]
    cap = slots // n_dp
    per = TILE // cap
    groups = slots // TILE
    experts = n_dp
    quarter = ff // 4
    size_t = TILE * 3 // 2
    hd = 64
    d = lax.axis_index("dp")
    h = lax.axis_index("head")
    sib, cross = (d, flip(h, 1)), (d, flip(h, 2))
    loads = [pltpu.make_async_copy(down_h.at[0], down, ld.at[0]), pltpu.make_async_copy(up_h.at[0], up, ld.at[1])]
    for copy in loads:
        copy.start()
    barrier_signal([(d, flip(h, k)) for k in (1, 2, 3)] + [(flip(d, r), h) for r in range(1, n_dp)])

    proj = projf[...].reshape(width, width)
    for i in range(tok // TILE):
        heads = []
        for b in range(4):
            heads += unpack(ctxf[b, i * size_t : (i + 1) * size_t, :])
        at = slice(i * TILE, (i + 1) * TILE)
        res[at, :] = x_ref[at, :].astype(F32) + dot(jnp.concatenate(heads, axis=1), proj) + pb_ref[...][None, :]
    gain, bias = g2_ref[...][None, :], b2_ref[...][None, :]
    chunk = 64

    def norm_rows(i, carry):
        at = pl.ds(pl.multiple_of(i * chunk, chunk), chunk)
        residual = res[at, :]
        average = jnp.mean(residual, axis=-1, keepdims=True)
        centred = residual - average
        inverse = lax.rsqrt(jnp.mean(centred * centred, axis=-1, keepdims=True) + EPSILON)
        stat[0, at, :] = average
        stat[1, at, :] = inverse
        normed = centred * inverse * gain + bias
        high = normed.astype(BF16)
        nhigh[at, :] = high
        nlow[at, :] = (normed - high.astype(F32)).astype(BF16)
        return carry

    lax.fori_loop(0, tok // chunk, norm_rows, 0)

    router3 = jnp.concatenate(split3(rt_ref[...]), axis=0)
    logits = fold3(dot(router3, nhigh[...], ((1,), (1,))) + dot(router3, nlow[...], ((1,), (1,))))
    raised = jnp.exp(logits - jnp.max(logits, axis=0, keepdims=True))
    prob = raised / jnp.sum(raised, axis=0, keepdims=True)
    hot, flat_row, slot_row = slot_layouts(routes_ref[...], experts, cap)
    gate_row = jnp.sum(prob * hot, axis=0, keepdims=True)
    gate_o[...] = row_to_col(gate_row)
    fraction = jnp.mean(hot, axis=1, keepdims=True)
    bal_o[...] = experts * jnp.sum(fraction * jnp.mean(prob, axis=1, keepdims=True), axis=0, keepdims=True)

    expert_row = jnp.sum(hot * lax.broadcasted_iota(jnp.int32, hot.shape, 0).astype(F32), axis=0, keepdims=True)
    other_row = jnp.bitwise_xor(expert_row.astype(jnp.int32), d)
    flat_x = other_row * cap + slot_row
    at_slot = (slot_row == lax.broadcasted_iota(jnp.int32, (128, tok), 0)).astype(F32).astype(BF16)
    other_hot = (other_row == lax.broadcasted_iota(jnp.int32, hot.shape, 0)).astype(F32)
    gates3 = jnp.concatenate([other_hot * part.astype(F32) for part in split3(gate_row)], axis=0).astype(BF16)
    gates = fold3(dot(gates3, at_slot, ((1,), (1,))))
    barrier_wait(3 + n_dp - 1)
    order = far_first(n_dp)

    def slot_block(r):
        return pl.ds(pl.multiple_of(r * cap, cap), cap)

    def send_rows(r):
        at = slot_block(r)
        return remote(disp.at[at, :], rows.at[at, :], ra_s.at[r], ra_r.at[r], (differ(d, r, n_dp), h))

    def send_gate(r):
        return remote(gsend.at[r], grecv.at[r], ga_s.at[r], ga_r.at[r], (differ(d, r, n_dp), h))

    slot_iota = lax.broadcasted_iota(jnp.int32, (cap, tok), 0)

    gates_s[...] = gates

    def fill(i, carry):
        r = lax.rem(i + n_dp // 2, n_dp)
        hits = (flat_x == slot_iota + r * cap).astype(F32).astype(BF16)
        gsend[r] = jnp.broadcast_to(gates_s[pl.ds(r, 1), :], (8, 128))
        block = dot(hits, nhigh[...]).astype(BF16)

        @pl.when(r != 0)
        def _():
            disp[slot_block(r), :] = block
            send_rows(r).start()
            send_gate(r).start()

        @pl.when(r == 0)
        def _():
            rows[:cap, :] = block
            grecv[0] = gsend[0]

        return carry

    lax.fori_loop(0, n_dp, fill, 0)

    loads[0].wait()

    def hidden_grad(i, carry):
        at = pl.ds(pl.multiple_of(lax.div(i, 4) * TILE, TILE), TILE)
        cols = pl.ds(pl.multiple_of(lax.rem(i, 4) * quarter, quarter), quarter)
        ghu[at, cols] = dot(cots[at, :], down[cols, :], ((1,), (1,))).astype(BF16)
        return carry

    lax.fori_loop(0, 4 * groups, hidden_grad, 0)
    loads[1].wait()

    step = quarter

    def send_back(r):
        at = slot_block(r)
        return remote(gin.at[at, :], ginr.at[at, :], rb_s.at[r], rb_r.at[r], (differ(d, r, n_dp), h))

    def send_gg(r):
        return remote(ggs.at[lax.div(r, per)], ggr.at[r], gb_s.at[r], gb_r.at[r], (differ(d, r, n_dp), h))

    def group_step(g, carry):
        for i in range(per):
            r = g * per + i

            @pl.when(r != 0)
            def _():
                send_rows(r).wait_recv()
                send_gate(r).wait_recv()

        at = pl.ds(pl.multiple_of(g * TILE, TILE), TILE)
        gate = jnp.concatenate([grecv[g * per + i].T[:cap, :1] for i in range(per)], axis=0)
        gacc[...] = jnp.zeros_like(gacc)
        gg[...] = jnp.zeros_like(gg)

        def expert(f, carry):
            cols = pl.ds(pl.multiple_of(f * step, step), step)
            u = dot(rows[at, :], up[:, cols]) + upb_ref[:, cols]
            share, density = gelu_parts(u)
            low = (u * share).astype(BF16)
            back = ghu[at, cols].astype(F32)
            hid[at, cols] = low
            meet = low.astype(F32) * back
            folded = meet[:, :128]
            for j in range(1, step // 128):
                folded += meet[:, j * 128 : (j + 1) * 128]
            gg[...] += folded
            pre = (gate * back * (share + u * density)).astype(BF16)
            ghu[at, cols] = pre
            gacc[...] += dot(pre, up[:, cols], ((1,), (1,)))
            return carry

        lax.fori_loop(0, ff // step, expert, 0)
        gin[at, :] = gacc[...].astype(BF16)
        cot_g = cots[at, :].astype(F32)
        gg_col = jnp.sum(gg[...], axis=1, keepdims=True) + jnp.sum(cot_g * downb_ref[...], axis=1, keepdims=True)
        ggs[g] = col_to_rows(gg_col)
        for i in range(per):
            r = g * per + i

            @pl.when(r != 0)
            def _():
                send_back(r).start()
                send_gg(r).start()

        cots[at, :] = (gate * cot_g).astype(BF16)
        rowst[:, at] = flip_t(rows[at, :])
        return carry

    lax.fori_loop(0, groups, group_step, 0)
    ginr[:cap, :] = gin[:cap, :]
    ggr[0] = ggs[0]

    third = quarter // 3

    def block_cols(index):
        return pl.ds(pl.multiple_of(index * quarter, quarter), quarter)

    def down_block(index, ref):
        def body(i, carry):
            cols = pl.ds(pl.multiple_of(index * quarter + i * third, third), third)
            ref[pl.ds(pl.multiple_of(i * third, third), third), :] = dot(hid[:, cols], cots[...], ((0,), (0,))).astype(BF16)
            return carry

        lax.fori_loop(0, 3, body, 0)

    def up_block(index, ref):
        part = width // 3

        def body(i, carry):
            at = pl.ds(pl.multiple_of(i * part, part), part)
            ref[at, :] = dot(rowst[at, :], ghu[:, block_cols(index)]).astype(BF16)
            return carry

        lax.fori_loop(0, 3, body, 0)

    def add_into(ref, other):
        def body(i, carry):
            at = pl.ds(pl.multiple_of(i * 64, 64), 64)
            ref[at, :] = (ref[at, :].astype(F32) + other[at, :].astype(F32)).astype(BF16)
            return carry

        lax.fori_loop(0, ref.shape[0] // 64, body, 0)

    down_sib = [remote(dsend.at[i], drecv.at[i], ds_s.at[i], ds_r.at[i], sib) for i in range(2)]
    down_cross = remote(dacc, dnr_o, ds_s.at[2], ds_r.at[2], cross)
    up_sib = [remote(dsend.at[i], urecv.at[i], us_s.at[i], us_r.at[i], sib) for i in range(2)]
    down_block(flip(h, 3), dsend.at[1])
    down_sib[1].start()
    down_block(flip(h, 2), dacc)
    down_sib[1].wait_recv()
    add_into(dacc, drecv.at[1])
    down_cross.start()
    down_block(flip(h, 1), dsend.at[0])
    down_sib[0].start()
    for r in order:
        send_rows(r).wait_send()

    def produce(i, carry):
        at = pl.ds(pl.multiple_of(i * TILE, TILE), TILE)
        disp[at, :] = (dot(hid[at, :], down[...]) + downb_ref[...]).astype(BF16)
        return carry

    lax.fori_loop(0, groups, produce, 0)
    prod_copy = pltpu.make_async_copy(disp, prod_o, out_sem.at[0])
    prod_copy.start()
    for copy in down_sib:
        copy.wait_send()
    up_block(flip(h, 3), dsend.at[1])
    up_sib[1].start()
    up_block(flip(h, 1), dsend.at[0])
    up_sib[0].start()
    up_block(flip(h, 2), upc_o)
    up_block(h, upo_o)
    down_block(h, dno_o)
    ones = jnp.ones((8, slots), BF16)
    up_bias = dot(ones, ghu[...])
    down_bias = dot(ones, cots[...])
    short = width // 4
    for b in range(4):
        bg_o[b, 0:1, :] = up_bias[:1, b * quarter : (b + 1) * quarter]
        bg_o[b, 1:2, :short] = down_bias[:1, b * short : (b + 1) * short]
    up_sib[1].wait_recv()
    add_into(upc_o, urecv.at[1])
    up_sib[0].wait_recv()
    add_into(upo_o, urecv.at[0])
    down_sib[0].wait_recv()
    add_into(dno_o, drecv.at[0])

    flat_col = row_to_col(flat_x.astype(F32)).astype(jnp.int32)
    for r in order:
        send_gg(r).wait_recv()
    slot_gg = [ggr[r][:1, (r % per) * cap : (r % per) * cap + cap] for r in range(n_dp)]
    slot_gg = jnp.concatenate(slot_gg, axis=0)
    grad_gate = jnp.sum(
        fold3(dot(jnp.concatenate(split3(slot_gg), axis=0), at_slot[:cap])) * other_hot, axis=0, keepdims=True
    )
    grad_prob = hot * grad_gate + (BAL_COEF * experts / tok) * fraction
    grad_logits = prob * (grad_prob - jnp.sum(prob * grad_prob, axis=0, keepdims=True))
    high, middle, low = split3(grad_logits)
    grads3 = jnp.concatenate([high, middle, low], axis=0)
    r_high, r_middle, r_low = split3(rt_ref[...])
    inner = 6 * experts
    padded = -(-inner // 128) * 128
    left = [v.astype(F32) for v in (high, high, high, middle, middle, low)]
    left = jnp.concatenate(left + [jnp.zeros((padded - inner, tok), F32)], axis=0).T.astype(BF16)
    right = jnp.concatenate([r_high, r_middle, r_low, r_high, r_middle, r_high, jnp.zeros((padded - inner, width), BF16)], axis=0)
    sm_o[...] = jnp.zeros_like(sm_o)
    sm_o[8 : 8 + experts, :] = fold3(dot(grads3, nhigh[...]) + dot(grads3, nlow[...]))
    for r in order:
        send_back(r).wait_recv()
    left_s[...] = left
    fcol[...] = flat_col
    part = 128

    def finish(i, carry):
        gain_sum, bias_sum, res_sum = carry
        at = pl.ds(pl.multiple_of(i * part, part), part)
        pick = (fcol[at, :] == lax.broadcasted_iota(jnp.int32, (part, slots), 1)).astype(F32).astype(BF16)
        grad_normed = dot(pick, ginr[...]) + dot(left_s[at, :], right)
        inverse = stat[1, at, :]
        scaled = (res[at, :] - stat[0, at, :]) * inverse
        grad_res = cot_ref[at, :].astype(F32) + norm_backward(grad_normed, scaled, inverse, gain)
        gres_o[at, :] = grad_res
        low_s[at, :] = grad_res.astype(BF16)
        return (
            gain_sum + jnp.sum(grad_normed * scaled, axis=0, keepdims=True),
            bias_sum + jnp.sum(grad_normed, axis=0, keepdims=True),
            res_sum + jnp.sum(grad_res, axis=0, keepdims=True),
        )

    gain_sum, bias_sum, res_sum = lax.fori_loop(0, tok // part, finish, (jnp.zeros((1, width), F32),) * 3)

    def turn_back(i, carry):
        back = dot(low_s[pl.ds(pl.multiple_of(i * TILE, TILE), TILE), :], proj, ((1,), (1,)))
        for b in range(4):
            outs = [back[:, (3 * b + a) * hd : (3 * b + a + 1) * hd] for a in range(3)]
            gctx_o[b, pl.ds(pl.multiple_of(i * size_t, size_t), size_t), :] = pack(outs).astype(BF16)
        return carry

    lax.fori_loop(0, tok // TILE, turn_back, 0)
    sm_o[0:1, :] = gain_sum
    sm_o[1:2, :] = bias_sum
    sm_o[2:3, :] = res_sum
    down_cross.wait()
    for copy in up_sib:
        copy.wait_send()
    for r in order:
        send_gate(r).wait_send()
        send_back(r).wait_send()
        send_gg(r).wait_send()
    prod_copy.wait()


def stage_m(n_dp, x, ctxf, projf, pb, g2, b2, router, routes, cot, cots, up, upb, down, downb):
    tok, width = x.shape
    slots = cots.shape[0]
    ff = up.shape[2]
    groups = slots // TILE
    quarter = ff // 4
    sds = jax.ShapeDtypeStruct
    vm = pltpu.VMEM
    return pl.pallas_call(
        functools.partial(kernel_m, n_dp),
        out_shape=(
            sds((tok, width), F32),
            sds((tok, 1), F32),
            sds((slots, width), BF16),
            sds((tok, width), F32),
            sds(ctxf.shape, BF16),
            sds((width, quarter), BF16),
            sds((width, quarter), BF16),
            sds((quarter, width), BF16),
            sds((quarter, width), BF16),
            sds((8 + n_dp, width), F32),
            sds((4, 8, quarter), F32),
            sds((1, 1), F32),
        ),
        in_specs=[VM] * 10 + [ANY, VM, ANY, VM],
        out_specs=(VM, VM, ANY, VM, VM, VM, VM, VM, ANY, VM, VM, VM),
        scratch_shapes=[
            vm((2, tok, 1), F32),
            vm((tok, width), BF16),
            vm((tok, width), BF16),
            vm((tok, width), BF16),
            vm((n_dp, 128), F32),
            vm((tok, -(-6 * n_dp // 128) * 128), BF16),
            vm((tok, 1), jnp.int32),
            vm((slots, width), BF16),
            vm((n_dp, 8, 128), F32),
            vm((slots, width), BF16),
            vm((width, slots), BF16),
            vm((n_dp, 8, 128), F32),
            vm((width, ff), BF16),
            vm((ff, width), BF16),
            vm((slots, ff), BF16),
            vm((slots, ff), BF16),
            vm((TILE, 128), F32),
            vm((TILE, width), F32),
            vm((slots, width), BF16),
            vm((groups, 8, TILE), F32),
            vm((slots, width), BF16),
            vm((n_dp, 8, TILE), F32),
            vm((2, quarter, width), BF16),
            vm((quarter, width), BF16),
            vm((2, quarter, width), BF16),
            vm((2, width, quarter), BF16),
            DMA((2,)), DMA((n_dp,)), DMA((n_dp,)), DMA((n_dp,)), DMA((n_dp,)), DMA((n_dp,)), DMA((n_dp,)),
            DMA((n_dp,)), DMA((n_dp,)), DMA((3,)), DMA((3,)), DMA((2,)), DMA((2,)), DMA((1,)),
        ],
        compiler_params=pltpu.CompilerParams(collective_id=1, has_side_effects=True, vmem_limit_bytes=VMEM_LIMIT),
    )(x, ctxf, projf, pb, g2, b2, router.T, routes.T, cot, cots, up, upb, down, downb)


def pack(outs):
    half = outs[2].shape[0] // 2
    return jnp.concatenate(
        [jnp.concatenate(outs[:2], axis=1), jnp.concatenate([outs[2][:half], outs[2][half:]], axis=1)], axis=0
    )


def unpack(tile):
    rows = tile.shape[0] * 2 // 3
    third = jnp.concatenate([tile[rows:, :64], tile[rows:, 64:]], axis=0)
    return [tile[:rows, :64], tile[:rows, 64:], third]


def unpack_t(tile):
    rows = tile.shape[1] * 2 // 3
    third = jnp.concatenate([tile[:64, rows:], tile[64:, rows:]], axis=1)
    return [tile[:64, :rows], tile[64:, :rows], third]


def flip_t(value):
    return value.astype(F32).T.astype(BF16)


def kernel_b(
    n_dp, gctx, qkv_h, p_h, ctx, ctxf, gath_h, w_ref, x_ref, g1_ref, b1_ref, gres, res, gate_ref, routes_ref, prod_h, upc_h, sm_ref, bg_ref,
    mixed_o, igrad_o, upr_o, comb_o, qb_o, sums_o, ends_o, bgs_o,
    gcr, qkv, p_v, gath, prodr, g_s, gt_s, qt_s, delta_s, dq_s, own_s, fcol, dkt, dvt, grads, gradst, gsend, gacc, grecv, comb, combx, comba, combr, pg, pgr, low_s,
    qb, qbr, smr, smd, smt, en, enr, ent, enq, bgr,
    ld, p_sem, gc_s, gc_r, pr_s, pr_r, uc_s, uc_r, gn_s, gn_r, gx_s, gx_r, qx_s, qx_r, qg_s, qg_r, pg_s, pg_r, qb_s, qb_r,
    sh_s, sh_r, sd_s, sd_r, eh_s, eh_r, ed_s, ed_r, bg_s, bg_r,
):
    tok, width = x_ref.shape
    heads, group, hd = qkv.shape[1:]
    cols = heads * hd
    tiles = group // TILE
    reach = group // 2 // TILE + 1
    per_block = tok // TILE
    slots = prod_h.shape[0]
    cap = slots // n_dp
    share = width // n_dp
    size_t = TILE * 3 // 2
    d = lax.axis_index("dp")
    h = lax.axis_index("head")
    sib, cross = (d, flip(h, 1)), (d, flip(h, 2))
    order = far_first(n_dp)

    def at_head(k):
        return (d, flip(h, k))

    def at_dp(r):
        return (flip(d, r), h)

    def p_load(t, size):
        return pltpu.make_async_copy(p_h.at[:, t, :, pl.ds(0, size)], p_v.at[t, :, :, pl.ds(0, size)], p_sem.at[t])

    barrier_signal([at_head(k) for k in (1, 2, 3)] + [at_dp(r) for r in range(1, n_dp)])
    load_qkv = pltpu.make_async_copy(qkv_h, qkv, ld.at[0])
    load_qkv.start()
    for t in range(tiles):
        p_load(t, min(t + 1, reach) * TILE).start()
    load_gath = pltpu.make_async_copy(gath_h, gath, ld.at[1])
    load_gath.start()
    dkt[...] = jnp.zeros_like(dkt)
    dvt[...] = jnp.zeros_like(dvt)
    barrier_wait(3 + n_dp - 1)

    def send_ctx(k):
        return remote(gctx.at[flip(h, k)], gcr.at[h], gc_s.at[k], gc_r.at[k], at_head(k))

    for k in (2, 3, 1):
        send_ctx(k).start()

    def send_prod(r):
        rows = pl.ds(r * cap, cap)
        return remote(prod_h.at[rows, :], prodr.at[rows, :], pr_s.at[r], pr_r.at[r], at_dp(r))

    for r in order:
        send_prod(r).start()
    prod_own = pltpu.make_async_copy(prod_h.at[pl.ds(0, cap), :], prodr.at[pl.ds(0, cap), :], pr_s.at[0])
    prod_own.start()
    gcr[h] = gctx[h]

    sm_head = [remote(sm_ref, smr.at[k], sh_s.at[k], sh_r.at[k], at_head(k)) for k in (1, 2, 3)]
    bg_head = [remote(bg_ref.at[flip(h, k)], bgr.at[k], bg_s.at[k], bg_r.at[k], at_head(k)) for k in (1, 2, 3)]
    up_half = width // 2
    up_cross = [
        remote(upc_h.at[pl.ds(i * up_half, up_half), :], upr_o.at[pl.ds(i * up_half, up_half), :], uc_s.at[i], uc_r.at[i], cross)
        for i in range(2)
    ]

    low_t = gres[...].T.astype(BF16)

    low_s[...] = low_t

    def proj_block(i, carry):
        index = differ(h, 3 - i, 4)
        total = []
        for j in range(per_block):
            outs = unpack(ctxf[index, j * size_t : (j + 1) * size_t, :])
            total.append(jnp.concatenate(outs, axis=1))
        out = dot(low_s[...], jnp.concatenate(total, axis=0))
        pg[3 - i] = pack([out[:, a * hd : (a + 1) * hd] for a in range(heads)]).astype(BF16)
        return carry

    lax.fori_loop(0, 4, proj_block, 0)
    pg_sib = [remote(pg.at[1 + 2 * i], pgr.at[i], pg_s.at[i], pg_r.at[i], sib) for i in range(2)]
    pg_sib[1].start()
    pg_sib[0].start()
    pg_cross = remote(pg.at[2], pgr.at[2], pg_s.at[2], pg_r.at[2], cross)
    pg_sib[1].wait_recv()
    pg[2] = (pg[2].astype(F32) + pgr[1].astype(F32)).astype(BF16)
    pg_cross.start()
    for copy in sm_head + bg_head:
        copy.start()
    load_qkv.wait()

    def wait_block(b):
        for k in (1, 2, 3):

            @pl.when(flip(h, k) == b)
            def _():
                remote(gctx.at[0], gcr.at[b], gc_s.at[k], gc_r.at[k], at_head(k)).wait_recv()

    def attention(t, size, unrolled):
        b, sub = lax.div(t, per_block), lax.rem(t, per_block)

        @pl.when(sub == 0)
        def _():
            wait_block(b)

        p_load(t, size).wait()
        rows = pl.ds(pl.multiple_of(t * TILE, TILE), TILE)
        win = pl.ds(pl.multiple_of((t + 1) * TILE - size, TILE), size)
        grad = gcr[b, pl.ds(pl.multiple_of(sub * size_t, size_t), size_t), :]
        meets = unpack(grad.astype(F32) * ctx[t].astype(F32))
        gs, gts = unpack(grad), unpack_t(flip_t(grad))
        qts = unpack_t(flip_t(pack([qkv[0, a, rows, :] for a in range(heads)])))
        for a in range(heads):
            delta_s[a] = jnp.sum(meets[a], axis=1, keepdims=True)
            g_s[a], gt_s[a], qt_s[a] = gs[a], gts[a], qts[a]

        def head(a, carry):
            p = p_v[t, a, :, :size]
            ds = (p.astype(F32) * (dot(g_s[a], qkv[2, a, win, :], ((1,), (1,))) - delta_s[a])).astype(BF16)
            dq_s[a] = dot(ds, qkv[1, a, win, :]) * (hd ** (-0.5))
            at = pl.ds(pl.multiple_of(a * hd, hd), hd)
            dkt[at, win] += dot(qt_s[a], ds)
            dvt[at, win] += dot(gt_s[a], p)
            return carry

        if unrolled:
            for a in range(heads):
                head(a, 0)
        else:
            lax.fori_loop(0, heads, head, 0)
        dq = jnp.concatenate([dq_s[a] for a in range(heads)], axis=1)
        grads[rows, :cols] = dq.astype(BF16)
        gradst[:cols, rows] = dq.T.astype(BF16)

    half = tiles // 2

    def both_halves(i, carry):
        @pl.when(i == 1)
        def _():
            up_cross[0].start()

        turn = lax.rem(i + lax.div(h, 2), 2)

        @pl.when(turn == 0)
        def _():
            for t in range(half):
                attention(t, (t + 1) * TILE, False)

        @pl.when(turn == 1)
        def _():
            def high_tile(t, inner):
                attention(t, reach * TILE, UNROLL_B)
                return inner

            lax.fori_loop(half, tiles, high_tile, 0)

        return carry

    lax.fori_loop(0, 2, both_halves, 0)

    def settle(t, carry):
        at = pl.ds(pl.multiple_of(t * TILE, TILE), TILE)
        both = jnp.concatenate([dkt[:, at], dvt[:, at]], axis=0)
        gradst[cols:, at] = both.astype(BF16)
        grads[at, cols:] = both.T.astype(BF16)
        return carry

    lax.fori_loop(0, tiles, settle, 0)

    pieces = 2
    piece = tok // pieces

    def normed_piece(index, i):
        at = pl.ds(pl.multiple_of(index * tok + i * piece, piece), piece)
        total = dot(grads[at, :cols], w_ref[0])
        for c in range(1, 3):
            total += dot(grads[at, c * cols : (c + 1) * cols], w_ref[c])
        return total

    def part(i):
        return pl.ds(pl.multiple_of(i * piece, piece), piece)

    def gn_sib(j, i):
        return remote(gsend.at[j, part(i), :], grecv.at[j, part(i), :], gn_s.at[j, i], gn_r.at[j, i], sib)

    def gn_cross(i):
        return remote(gacc.at[part(i), :], grecv.at[2, part(i), :], gx_s.at[i], gx_r.at[i], cross)

    def across(i, carry):
        gsend[1, part(i), :] = normed_piece(flip(h, 3), i).astype(BF16)
        gn_sib(1, i).start()
        mine = normed_piece(flip(h, 2), i)
        gn_sib(1, i).wait_recv()
        gacc[part(i), :] = (mine + grecv[1, part(i), :].astype(F32)).astype(BF16)
        gn_cross(i).start()
        return carry

    lax.fori_loop(0, pieces, across, 0)

    def beside(i, carry):
        gsend[0, part(i), :] = normed_piece(flip(h, 1), i).astype(BF16)
        gn_sib(0, i).start()
        own_s[part(i), :] = normed_piece(h, i)
        return carry

    lax.fori_loop(0, pieces, beside, 0)

    pg_sib[0].wait_recv()
    pg_cross.wait_recv()
    done = unpack(pg[0].astype(F32) + pgr[0].astype(F32) + pgr[2].astype(F32))
    comb[:, 3 * cols :] = jnp.concatenate(done, axis=1).astype(BF16)
    load_gath.wait()
    for c in range(3):
        comb[:, c * cols : (c + 1) * cols] = dot(gradst[c * cols : (c + 1) * cols, :], gath[...]).T.astype(BF16)
    ones = jnp.ones((8, group), BF16)
    qb[...] = jnp.concatenate([dot(ones, grads[:, :cols])[:1], dot(ones, grads[:, 2 * cols :])[:1]], axis=1)

    pairs = n_dp // 2
    side, place = lax.rem(d, 2), lax.div(d, 2)

    def comb_rows(index):
        return pl.ds(pl.multiple_of(index * share, share), share)

    def send_side(j):
        return remote(comb.at[comb_rows(2 * j + 1 - side), :], combx.at[j], qx_s.at[j], qx_r.at[j], at_dp(1))

    def send_qg(r):
        return remote(comba.at[flip(place, r)], combr.at[r], qg_s.at[r], qg_r.at[r], at_dp(2 * r))

    def send_qb(r):
        return remote(qb, qbr.at[r], qb_s.at[r], qb_r.at[r], at_dp(r))

    pair_order = list(range(pairs // 2, pairs)) + list(range(1, pairs // 2))
    for j in range(pairs):
        send_side(j).start()
    for r in order:
        send_qb(r).start()
    for copy in sm_head:
        copy.wait_recv()
    total = sm_ref[...] + smr[1] + smr[2] + smr[3]
    for e in range(n_dp):
        smt[e] = (pltpu.roll(total, width - e * share, 1) if e else total)[:, :128]

    def send_sm(r):
        return remote(smt.at[flip(d, r)], smd.at[r], sd_s.at[r], sd_r.at[r], at_dp(r))

    for r in order:
        send_sm(r).start()
    for j in range(pairs):
        send_side(j).wait_recv()
        comba[j] = (comb[comb_rows(2 * j + side), :].astype(F32) + combx[j].astype(F32)).astype(BF16)
    for r in pair_order:
        send_qg(r).start()

    hot, flat_row, slot_row = slot_layouts(routes_ref[...], n_dp, cap)
    expert_row = jnp.sum(hot * lax.broadcasted_iota(jnp.int32, hot.shape, 0).astype(F32), axis=0, keepdims=True)
    flat_x = jnp.bitwise_xor(expert_row.astype(jnp.int32), d) * cap + slot_row
    flat_col = row_to_col(flat_x.astype(F32)).astype(jnp.int32)
    for r in order:
        send_prod(r).wait_recv()
    prod_own.wait()
    fcol[...] = flat_col

    def mix(i, carry):
        at = pl.ds(pl.multiple_of(i * 128, 128), 128)
        pick = (fcol[at, :] == lax.broadcasted_iota(jnp.int32, (128, slots), 1)).astype(F32).astype(BF16)
        mixed_o[at, :] = (res[at, :] + gate_ref[at, :] * dot(pick, prodr[...])).astype(BF16)
        return carry

    lax.fori_loop(0, tok // 128, mix, 0)
    gain, bias = g1_ref[...][None, :], b1_ref[...][None, :]

    def norm_back(i, carry):
        at = pl.ds(pl.multiple_of(i * 64, 64), 64)
        own = own_s[at, :] + grecv[0, at, :].astype(F32) + grecv[2, at, :].astype(F32)
        _, scaled, inverse = normalize(x_ref[at, :].astype(F32), gain, bias)
        igrad_o[at, :] = gres[at, :] + norm_backward(own, scaled, inverse, gain)
        return (carry[0] + jnp.sum(own * scaled, axis=0, keepdims=True), carry[1] + jnp.sum(own, axis=0, keepdims=True))

    sums = (jnp.zeros((1, width), F32),) * 2
    for i in range(pieces):
        gn_sib(0, i).wait_recv()
        gn_cross(i).wait_recv()
        sums = lax.fori_loop(i * (piece // 64), (i + 1) * (piece // 64), norm_back, sums)
    gain_sum, bias_sum = sums
    en[0:1, :] = gain_sum
    en[1:2, :] = bias_sum
    en_head = [remote(en, enr.at[k], eh_s.at[k], eh_r.at[k], at_head(k)) for k in (1, 2, 3)]
    for copy in en_head:
        copy.start()
    up_cross[1].start()
    for copy in en_head:
        copy.wait_recv()
    ent[...] = en[...] + enr[1] + enr[2] + enr[3]
    en_dp = [remote(ent, enq.at[r], ed_s.at[r], ed_r.at[r], at_dp(r)) for r in range(1, n_dp)]
    for copy in en_dp:
        copy.start()

    for r in pair_order:
        send_qg(r).wait_recv()
    for r in order:
        send_qb(r).wait_recv()
        send_sm(r).wait_recv()
    total = comb[comb_rows(d), :].astype(F32) + combx[place].astype(F32)
    for r in range(1, pairs):
        total += combr[r].astype(F32)
    comb_o[...] = total
    sums = qb[...]
    for r in range(1, n_dp):
        sums += qbr[r]
    qb_o[...] = sums
    total = smt[d]
    for r in range(1, n_dp):
        total += smd[r]
    sums_o[...] = total
    for copy in bg_head:
        copy.wait_recv()
    bgs_o[...] = bg_ref[h] + bgr[1] + bgr[2] + bgr[3]
    for copy in en_dp:
        copy.wait_recv()
    total = ent[...]
    for r in range(1, n_dp):
        total += enq[r]
    ends_o[...] = total

    for k in (1, 2, 3):
        send_ctx(k).wait_send()
    for r in order:
        send_prod(r).wait_send()
        send_qb(r).wait_send()
        send_sm(r).wait_send()
    for r in pair_order:
        send_qg(r).wait_send()
    for j in range(pairs):
        send_side(j).wait_send()
    for copy in up_cross:
        copy.wait()
    pg_cross.wait_send()
    for copy in pg_sib + [gn_cross(i) for i in range(pieces)] + [gn_sib(j, i) for j in range(2) for i in range(pieces)] + sm_head + bg_head + en_head + en_dp:
        copy.wait_send()


def stage_b(n_dp, gctx, qkv, probs, ctx, ctxf, gath, w, x, g1, b1, gres, res, gate, routes, prod, upc, sm, bg):
    tok, width = x.shape
    _, heads, group, hd = qkv.shape
    cols = heads * hd
    span = probs.shape[3]
    share = width // n_dp
    sds = jax.ShapeDtypeStruct
    vm = pltpu.VMEM
    packed = width * 3 // 2
    return pl.pallas_call(
        functools.partial(kernel_b, n_dp),
        out_shape=(
            sds((tok, width), BF16),
            sds((tok, width), F32),
            sds(upc.shape, BF16),
            sds((share, width), F32),
            sds((1, 2 * cols), F32),
            sds((sm.shape[0], 128), F32),
            sds((2, width), F32),
            sds(bg.shape[1:], F32),
        ),
        in_specs=[VM, ANY, ANY, VM, VM, ANY] + [VM] * 8 + [ANY, ANY, VM, VM],
        out_specs=(VM, VM, ANY) + (VM,) * 5,
        scratch_shapes=[
            vm(gctx.shape, BF16), vm((3, heads, group, hd), BF16), vm((group // TILE, heads, TILE, span), BF16), vm((group, width), BF16),
            vm(prod.shape, BF16),
            vm((heads, TILE, hd), BF16), vm((heads, hd, TILE), BF16), vm((heads, hd, TILE), BF16), vm((heads, TILE, 1), F32),
            vm((heads, TILE, hd), F32), vm((tok, width), F32), vm((tok, 1), jnp.int32), vm((cols, group), F32), vm((cols, group), F32), vm((group, 3 * cols), BF16), vm((3 * cols, group), BF16),
            vm((2, tok, width), BF16), vm((tok, width), BF16), vm((3, tok, width), BF16),
            vm((width, 4 * cols), BF16), vm((n_dp // 2, share, 4 * cols), BF16), vm((n_dp // 2, share, 4 * cols), BF16),
            vm((n_dp // 2, share, 4 * cols), BF16),
            vm((4, packed, 128), BF16), vm((3, packed, 128), BF16), vm((width, tok), BF16),
            vm((1, 2 * cols), F32), vm((n_dp, 1, 2 * cols), F32),
            vm((4,) + sm.shape, F32), vm((n_dp, sm.shape[0], 128), F32), vm((n_dp, sm.shape[0], 128), F32),
            vm((2, width), F32), vm((4, 2, width), F32), vm((2, width), F32), vm((n_dp, 2, width), F32),
            vm((4,) + bg.shape[1:], F32),
            DMA((2,)), DMA((group // TILE,)), DMA((4,)), DMA((4,)), DMA((n_dp,)), DMA((n_dp,)), DMA((2,)), DMA((2,)), DMA((2, 2)), DMA((2, 2)),
            DMA((2,)), DMA((2,)), DMA((n_dp // 2,)), DMA((n_dp // 2,)), DMA((n_dp // 2,)), DMA((n_dp // 2,)), DMA((3,)), DMA((3,)),
            DMA((n_dp,)), DMA((n_dp,)),
            DMA((4,)), DMA((4,)), DMA((n_dp,)), DMA((n_dp,)), DMA((4,)), DMA((4,)), DMA((n_dp,)), DMA((n_dp,)), DMA((4,)), DMA((4,)),
        ],
        compiler_params=pltpu.CompilerParams(collective_id=2, has_side_effects=True, vmem_limit_bytes=VMEM_LIMIT),
    )(gctx, qkv, probs, ctx, ctxf, gath, w.transpose(0, 2, 1), x, g1, b1, gres, res, gate, routes.T, prod, upc, sm, bg)


def kernel_f(
    n_dp, mixed, igrad, upo, upr, dno, dnr, comb, qb, sums, ends, bgs, bal,
    mixed_o, bal_o, igrad_o, g1_o, b1_o, qkv_o, qkvb_o, proj_o, pb_o, g2_o, b2_o, router_o, up_o, upb_o, down_o, downb_o,
):
    mixed_o[...] = mixed[...]
    igrad_o[...] = igrad[...]
    up_o[0] = upo[...].astype(F32) + upr[...].astype(F32)
    down_o[0] = dno[...].astype(F32) + dnr[...].astype(F32)

    @pl.when(pl.program_id(0) == 0)
    def _():
        d = lax.axis_index("dp")
        device = d * 4 + lax.axis_index("head")
        width = ends.shape[1]
        part = g1_o.shape[0]
        cols = qkv_o.shape[2]
        hd = cols // 3
        share = qkvb_o.shape[2]
        bal_o[...] = bal[0]
        shift = lax.rem(width - device * part, width)
        mine = pltpu.roll(sums[...], lax.rem(128 - lax.axis_index("head") * part, 128), 1)[:, :part]
        tail = pltpu.roll(jnp.concatenate([ends[...], jnp.zeros((6, width), F32)], axis=0), shift, 1)[:, :part]
        g1_o[...] = tail[0]
        b1_o[...] = tail[1]
        g2_o[...] = mine[0]
        b2_o[...] = mine[1]
        pb_o[...] = mine[2]
        router_o[...] = mine[8 : 8 + n_dp]
        for c in range(3):
            qkv_o[c] = comb[:, c * cols : (c + 1) * cols]
        proj_o[...] = comb[:, 3 * cols :].T
        turned = pltpu.roll(jnp.broadcast_to(qb[...], (8, 2 * cols)), lax.rem(2 * cols - d * share, 2 * cols), 1)
        for a in range(3):
            for c in range(2):
                at = c * cols + a * hd
                qkvb_o[a, c : c + 1, :] = turned[:1, at : at + share]
        upb_o[...] = bgs[0:1, :]
        downb_o[...] = bgs[1:2, : downb_o.shape[1]]


def stage_f(n_dp, mixed, igrad, upo, upr, dno, dnr, comb, qb, sums, ends, bgs, bal):
    tok, width = mixed.shape
    cols = qb.shape[1] // 2
    part = width // (4 * n_dp)
    share = width // n_dp
    steps = 4
    sds = jax.ShapeDtypeStruct

    def rows(shape):
        if len(shape) == 3:
            return pl.BlockSpec((1, shape[1] // steps, shape[2]), lambda i: (0, i, 0))
        return pl.BlockSpec((shape[0] // steps, shape[1]), lambda i: (i, 0))

    def whole(shape):
        return pl.BlockSpec(shape, lambda i: (0,) * len(shape))

    args = (mixed, igrad, upo, upr, dno, dnr, comb, qb, sums, ends, bgs, bal)
    outs = (
        sds((tok, width), BF16), sds((1,), F32), sds((tok, width), F32), sds((part,), F32), sds((part,), F32),
        sds((3, share, cols), F32), sds((3, 2, cols // 3 // n_dp), F32), sds((cols, share), F32), sds((part,), F32), sds((part,), F32),
        sds((part,), F32), sds((n_dp, part), F32), sds((1,) + upo.shape, F32), sds((1, upo.shape[1]), F32),
        sds((1,) + dno.shape, F32), sds((1, width // 4), F32),
    )
    return pl.pallas_call(
        functools.partial(kernel_f, n_dp),
        out_shape=outs,
        grid=(steps,),
        in_specs=[rows(a.shape) for a in args[:6]] + [whole(a.shape) for a in args[6:]],
        out_specs=tuple(rows(o.shape) if i in (0, 2, 12, 14) else whole(o.shape) for i, o in enumerate(outs)),
        compiler_params=pltpu.CompilerParams(vmem_limit_bytes=VMEM_LIMIT),
    )(*args)


def local(
    block_input, norm1_gain, norm1_bias, qkv_weight, qkv_bias, proj_weight, proj_bias, norm2_gain, norm2_bias, router_weight,
    up_weight, up_bias, down_weight, down_bias, routes, lengths, cotangent,
):
    tok, width = block_input.shape
    experts = router_weight.shape[1]
    cap = 2 * tok // experts
    gath, qkv, probs, ctx, ctxf, projf, cots = stage_a(
        experts, block_input, norm1_gain, norm1_bias, qkv_weight, qkv_bias, proj_weight, routes, cotangent, lengths, cap
    )
    res, gate, prod, gres, gctx, upc, upo, dno, dnr, sm, bg, balance = stage_m(
        experts, block_input, ctxf, projf, proj_bias, norm2_gain, norm2_bias, router_weight, routes, cotangent, cots,
        up_weight, up_bias, down_weight, down_bias,
    )
    mixed, igrad, upr, comb, qb, sums, ends, bgs = stage_b(
        experts, gctx, qkv, probs, ctx, ctxf, gath, qkv_weight, block_input, norm1_gain, norm1_bias, gres, res, gate, routes, prod,
        upc, sm, bg,
    )
    outs = list(stage_f(experts, mixed, igrad, upo, upr, dno, dnr, comb, qb, sums, ends, bgs, balance))
    outs[6] = outs[6].transpose(1, 0, 2)
    outs[11] = outs[11].T
    return tuple(outs)


def solution(mesh):
    placed = (
        P(("dp", "head"), None), P(), P(), P(None, None, "head"), P(None, "head", None), P("head", None), P(), P(), P(), P(),
        P("dp", None, None), P("dp", None), P("dp", None, None), P("dp", None), P(("dp", "head"), None), P("dp", None),
        P(("dp", "head"), None),
    )
    tokens = P(("dp", "head"))
    return jax.shard_map(
        local,
        mesh=mesh,
        in_specs=placed,
        out_specs=(
            P(("dp", "head"), None), tokens, P(("dp", "head"), None), tokens, tokens, P(None, "dp", "head"), P(None, "head", "dp"),
            P("head", "dp"), tokens, tokens, tokens, P(("dp", "head"), None), P("dp", None, "head"), P("dp", "head"),
            P("dp", "head", None), P("dp", "head"),
        ),
        check_vma=False,
    )
```

profile of v0, /device:TPU:0, one launch (start us, length us, event | category | flops | bytes accessed | tf_op | source)
XLA Modules:
  0.0 231.8 jit_solution(13064884091192466132)
XLA Ops:
  0.6 54.1 %shard_map.288 = (bf16[2048,768]{1,0:T(8,128)(2,1)}, bf16[3,3,2048,64]{3,2,1,0:T(8,128)(2,1)}, bf16[3,8,256,1280]{3,2,1,0:T(8,128)(2,1)}, bf16[8,384,128]{2,1,0:...) custom-call(bf16[512,768]{1,0:T(8,128)(2,1)} %x_ref.5, ...), custom_call_target="tpu_custom_call" | custom-call | tf_op jit(solution)/shard_map/pallas_call | solution.py:315
  54.8 86.2 %shard_map.289 = (f32[512,768]{1,0:T(8,128)}, f32[512,1]{1,0:T(8,128)}, bf16[1024,768]{1,0:T(8,128)(2,1)}, f32[512,768]{1,0:T(8,128)}, bf16[4,768,128]{2,1,0:T(8...) custom-call(bf16[512,768]{1,0:T(8,128)(2,1)} %x_ref.5, ...), custom_call_target="tpu_custom_call" | custom-call | tf_op jit(solution)/shard_map/pallas_call | solution.py:707
  140.9 83.1 %shard_map.290 = (bf16[512,768]{1,0:T(8,128)(2,1)}, f32[512,768]{1,0:T(8,128)}, bf16[768,768]{1,0:T(8,128)(2,1)}, f32[96,768]{1,0:T(8,128)}, f32[1,384]{1,0:T(1,...) custom-call(bf16[4,768,128]{2,1,0:T(8,128)(2,1)} %get-tuple-element.62.gctx, ...), custom_call_target="tpu_custom_call" | custom-call | tf_op jit(solution)/shard_map/pallas_call | solution.py:1135
  224.0 7.6 %shard_map.291 = (bf16[512,768]{1,0:T(8,128)(2,1)}, f32[1]{0:T(128)}, f32[512,768]{1,0:T(8,128)}, f32[24]{0:T(128)}, f32[24]{0:T(128)}, /*index=5*/f32[3,96,192]...) custom-call(bf16[512,768]{1,0:T(8,128)(2,1)} %get-tuple-element.74.m, ...), custom_call_target="tpu_custom_call" | custom-call | tf_op jit(solution)/shard_map/pallas_call | solution.py:1234
where the time goes:
time: 232 us
  Pallas kernels  231 us (100%)
    pallas_call x1, Pallas kernels, stage_m(): pl.pallas_call(functools.partial(kernel_m, n_dp), out_shape=(sds((tok, wi...  86.2 us
    pallas_call x1, Pallas kernels, stage_b(): pl.pallas_call(functools.partial(kernel_b, n_dp), out_shape=(sds((tok, wi...  83.1 us
    pallas_call x1, Pallas kernels, stage_a(): pl.pallas_call(functools.partial(kernel_a, n_dp), out_shape=(sds((group,...  54.1 us
    pallas_call x1, Pallas kernels, stage_f(): pl.pallas_call(functools.partial(kernel_f, n_dp), out_shape=outs, grid=(s...  7.59 us

commit v1 on v0

--- a/solution.py
+++ b/solution.py
@@ -14,9 +14,9 @@
 F32 = jnp.float32
 BF16 = jnp.bfloat16
 TILE = 256
-VMEM_LIMIT = 60 << 20
+VMEM_LIMIT = 61 << 20
 UNROLL_A = True
-UNROLL_B = False
+UNROLL_B = True
 
 
 def flip(index, bits):
@@ -380,8 +380,8 @@
 
 def kernel_m(
     n_dp, x_ref, ctxf, projf, pb_ref, g2_ref, b2_ref, rt_ref, routes_ref, cot_ref, cots, up_h, upb_ref, down_h, downb_ref,
-    res, gate_o, prod_o, gres_o, gctx_o, upc_o, upo_o, dno_o, dnr_o, sm_o, bg_o, bal_o,
-    stat, nhigh, nlow, low_s, gates_s, left_s, fcol, disp, gsend, rows, rowst, grecv, up, down, ghu, hid, gg, gacc, gin, ggs, ginr, ggr, dsend, dacc, drecv, urecv,
+    res_o, gate_o, prod_o, gres_o, gctx_o, upc_h, upo_h, dno_h, dnr_o, sm_o, bg_o, bal_o,
+    res, upc_o, upo_o, dno_o, stat, nhigh, nlow, low_s, gates_s, left_s, fcol, disp, gsend, rows, rowst, grecv, up, down, ghu, hid, gg, gacc, gin, ggs, ginr, ggr, dsend, dacc, drecv, urecv,
     ld, ra_s, ra_r, ga_s, ga_r, rb_s, rb_r, gb_s, gb_r, ds_s, ds_r, us_s, us_r, out_sem,
 ):
     tok, width = x_ref.shape
@@ -608,6 +608,11 @@
     lax.fori_loop(0, groups, produce, 0)
     prod_copy = pltpu.make_async_copy(disp, prod_o, out_sem.at[0])
     prod_copy.start()
+    outs = [
+        pltpu.make_async_copy(a, b, out_sem.at[1 + i])
+        for i, (a, b) in enumerate(((res, res_o), (upc_o, upc_h), (upo_o, upo_h), (dno_o, dno_h)))
+    ]
+    outs[0].start()
     for copy in down_sib:
         copy.wait_send()
     up_block(flip(h, 3), dsend.at[1])
@@ -626,10 +631,13 @@
         bg_o[b, 1:2, :short] = down_bias[:1, b * short : (b + 1) * short]
     up_sib[1].wait_recv()
     add_into(upc_o, urecv.at[1])
+    outs[1].start()
     up_sib[0].wait_recv()
     add_into(upo_o, urecv.at[0])
+    outs[2].start()
     down_sib[0].wait_recv()
     add_into(dno_o, drecv.at[0])
+    outs[3].start()
 
     flat_col = row_to_col(flat_x.astype(F32)).astype(jnp.int32)
     for r in order:
@@ -678,8 +686,8 @@
     def turn_back(i, carry):
         back = dot(low_s[pl.ds(pl.multiple_of(i * TILE, TILE), TILE), :], proj, ((1,), (1,)))
         for b in range(4):
-            outs = [back[:, (3 * b + a) * hd : (3 * b + a + 1) * hd] for a in range(3)]
-            gctx_o[b, pl.ds(pl.multiple_of(i * size_t, size_t), size_t), :] = pack(outs).astype(BF16)
+            heads = [back[:, (3 * b + a) * hd : (3 * b + a + 1) * hd] for a in range(3)]
+            gctx_o[b, pl.ds(pl.multiple_of(i * size_t, size_t), size_t), :] = pack(heads).astype(BF16)
         return carry
 
     lax.fori_loop(0, tok // TILE, turn_back, 0)
@@ -694,6 +702,8 @@
         send_back(r).wait_send()
         send_gg(r).wait_send()
     prod_copy.wait()
+    for copy in outs:
+        copy.wait()
 
 
 def stage_m(n_dp, x, ctxf, projf, pb, g2, b2, router, routes, cot, cots, up, upb, down, downb):
@@ -717,12 +727,13 @@
             sds((quarter, width), BF16),
             sds((quarter, width), BF16),
             sds((8 + n_dp, width), F32),
-            sds((4, 8, quarter), F32),
+            sds((4, 2, quarter), F32),
             sds((1, 1), F32),
         ),
         in_specs=[VM] * 10 + [ANY, VM, ANY, VM],
-        out_specs=(VM, VM, ANY, VM, VM, VM, VM, VM, ANY, VM, VM, VM),
+        out_specs=(ANY, VM, ANY, VM, VM, ANY, ANY, ANY, ANY, VM, VM, VM),
         scratch_shapes=[
+            vm((tok, width), F32), vm((width, quarter), BF16), vm((width, quarter), BF16), vm((quarter, width), BF16),
             vm((2, tok, 1), F32),
             vm((tok, width), BF16),
             vm((tok, width), BF16),
@@ -750,7 +761,7 @@
             vm((2, quarter, width), BF16),
             vm((2, width, quarter), BF16),
             DMA((2,)), DMA((n_dp,)), DMA((n_dp,)), DMA((n_dp,)), DMA((n_dp,)), DMA((n_dp,)), DMA((n_dp,)),
-            DMA((n_dp,)), DMA((n_dp,)), DMA((3,)), DMA((3,)), DMA((2,)), DMA((2,)), DMA((1,)),
+            DMA((n_dp,)), DMA((n_dp,)), DMA((3,)), DMA((3,)), DMA((2,)), DMA((2,)), DMA((5,)),
         ],
         compiler_params=pltpu.CompilerParams(collective_id=1, has_side_effects=True, vmem_limit_bytes=VMEM_LIMIT),
     )(x, ctxf, projf, pb, g2, b2, router.T, routes.T, cot, cots, up, upb, down, downb)
@@ -780,11 +791,11 @@
 
 
 def kernel_b(
-    n_dp, gctx, qkv_h, p_h, ctx, ctxf, gath_h, w_ref, x_ref, g1_ref, b1_ref, gres, res, gate_ref, routes_ref, prod_h, upc_h, sm_ref, bg_ref,
+    n_dp, gctx, qkv_h, p_h, ctx, ctxf, gath_h, w_h, x_h, g1_ref, b1_ref, gres, res_h, gate_ref, routes_ref, prod_h, upc_h, sm_ref, bg_ref,
     mixed_o, igrad_o, upr_o, comb_o, qb_o, sums_o, ends_o, bgs_o,
-    gcr, qkv, p_v, gath, prodr, g_s, gt_s, qt_s, delta_s, dq_s, own_s, fcol, dkt, dvt, grads, gradst, gsend, gacc, grecv, comb, combx, comba, combr, pg, pgr, low_s,
-    qb, qbr, smr, smd, smt, en, enr, ent, enq, bgr,
-    ld, p_sem, gc_s, gc_r, pr_s, pr_r, uc_s, uc_r, gn_s, gn_r, gx_s, gx_r, qx_s, qx_r, qg_s, qg_r, pg_s, pg_r, qb_s, qb_r,
+    w_ref, x_ref, res, gcr, qkv, p_v, gath, prodr, g_s, gt_s, qt_s, delta_s, dq_s, own_s, fcol, dkt, dvt, grads, gradst, gsend, gacc, grecv, comb, combx, comba, combr, ctxa, pgall, pgx, pga, pgz, pgh, pghr, low_s,
+    qb, qbr, smr, smd, smt, smh, en, enr, ent, enq, bgr,
+    ld, p_sem, gc_s, gc_r, pr_s, pr_r, uc_s, uc_r, gn_s, gn_r, gx_s, gx_r, qx_s, qx_r, qg_s, qg_r, px_s, px_r, pz_s, pz_r, ph_s, ph_r, qb_s, qb_r,
     sh_s, sh_r, sd_s, sd_r, eh_s, eh_r, ed_s, ed_r, bg_s, bg_r,
 ):
     tok, width = x_ref.shape
@@ -818,6 +829,25 @@
         p_load(t, min(t + 1, reach) * TILE).start()
     load_gath = pltpu.make_async_copy(gath_h, gath, ld.at[1])
     load_gath.start()
+    later = [pltpu.make_async_copy(a, b, ld.at[2 + i]) for i, (a, b) in enumerate(((w_h, w_ref), (x_h, x_ref), (res_h, res)))]
+    for copy in later:
+        copy.start()
+    low_s[...] = gres[...].T.astype(BF16)
+    for j in range(per_block):
+        outs = []
+        for b in range(4):
+            outs += unpack(ctxf[b, j * size_t : (j + 1) * size_t, :])
+        ctxa[j * TILE : (j + 1) * TILE, :] = jnp.concatenate(outs, axis=1)
+
+    def proj_rows(i, carry):
+        at = pl.ds(pl.multiple_of(i * TILE, TILE), TILE)
+        pgall[at, :] = dot(low_s[at, :], ctxa[...]).astype(BF16)
+        return carry
+
+    lax.fori_loop(0, width // TILE, proj_rows, 0)
+    sm_all = sm_ref[...]
+    for e in range(n_dp):
+        smt[e] = (pltpu.roll(sm_all, width - e * share, 1) if e else sm_all)[:, :128]
     dkt[...] = jnp.zeros_like(dkt)
     dvt[...] = jnp.zeros_like(dvt)
     barrier_wait(3 + n_dp - 1)
@@ -832,13 +862,31 @@
         rows = pl.ds(r * cap, cap)
         return remote(prod_h.at[rows, :], prodr.at[rows, :], pr_s.at[r], pr_r.at[r], at_dp(r))
 
+    pairs = n_dp // 2
+    side, place = lax.rem(d, 2), lax.div(d, 2)
+    pair_order = list(range(pairs // 2, pairs)) + list(range(1, pairs // 2))
+
+    def dp_rows(index):
+        return pl.ds(pl.multiple_of(index * share, share), share)
+
+    def send_px(j):
+        return remote(pgall.at[dp_rows(2 * j + 1 - side), :], pgx.at[j], px_s.at[j], px_r.at[j], at_dp(1))
+
+    def send_pz(r):
+        return remote(pga.at[flip(place, r)], pgz.at[r], pz_s.at[r], pz_r.at[r], at_dp(2 * r))
+
+    def send_ph(k):
+        return remote(pgh.at[flip(h, k)], pghr.at[k], ph_s.at[k], ph_r.at[k], at_head(k))
+
+    for j in range(pairs):
+        send_px(j).start()
     for r in order:
         send_prod(r).start()
     prod_own = pltpu.make_async_copy(prod_h.at[pl.ds(0, cap), :], prodr.at[pl.ds(0, cap), :], pr_s.at[0])
     prod_own.start()
     gcr[h] = gctx[h]
 
-    sm_head = [remote(sm_ref, smr.at[k], sh_s.at[k], sh_r.at[k], at_head(k)) for k in (1, 2, 3)]
+    sm_head = [remote(smh, smr.at[k], sh_s.at[k], sh_r.at[k], at_head(k)) for k in (1, 2, 3)]
     bg_head = [remote(bg_ref.at[flip(h, k)], bgr.at[k], bg_s.at[k], bg_r.at[k], at_head(k)) for k in (1, 2, 3)]
     up_half = width // 2
     up_cross = [
@@ -846,30 +894,15 @@
         for i in range(2)
     ]
 
-    low_t = gres[...].T.astype(BF16)
-
-    low_s[...] = low_t
-
-    def proj_block(i, carry):
-        index = differ(h, 3 - i, 4)
-        total = []
-        for j in range(per_block):
-            outs = unpack(ctxf[index, j * size_t : (j + 1) * size_t, :])
-            total.append(jnp.concatenate(outs, axis=1))
-        out = dot(low_s[...], jnp.concatenate(total, axis=0))
-        pg[3 - i] = pack([out[:, a * hd : (a + 1) * hd] for a in range(heads)]).astype(BF16)
-        return carry
-
-    lax.fori_loop(0, 4, proj_block, 0)
-    pg_sib = [remote(pg.at[1 + 2 * i], pgr.at[i], pg_s.at[i], pg_r.at[i], sib) for i in range(2)]
-    pg_sib[1].start()
-    pg_sib[0].start()
-    pg_cross = remote(pg.at[2], pgr.at[2], pg_s.at[2], pg_r.at[2], cross)
-    pg_sib[1].wait_recv()
-    pg[2] = (pg[2].astype(F32) + pgr[1].astype(F32)).astype(BF16)
-    pg_cross.start()
-    for copy in sm_head + bg_head:
+    for copy in bg_head:
         copy.start()
+
+    def send_sm(r):
+        return remote(smt.at[flip(d, r)], smd.at[r], sd_s.at[r], sd_r.at[r], at_dp(r))
+
+    for r in order:
+        send_sm(r).start()
+
     load_qkv.wait()
 
     def wait_block(b):
@@ -920,7 +953,8 @@
     def both_halves(i, carry):
         @pl.when(i == 1)
         def _():
-            up_cross[0].start()
+            for copy in up_cross:
+                copy.start()
 
         turn = lax.rem(i + lax.div(h, 2), 2)
 
@@ -940,6 +974,9 @@
         return carry
 
     lax.fori_loop(0, 2, both_halves, 0)
+
+    for copy in later:
+        copy.wait()
 
     def settle(t, carry):
         at = pl.ds(pl.multiple_of(t * TILE, TILE), TILE)
@@ -979,33 +1016,20 @@
         return carry
 
     lax.fori_loop(0, pieces, across, 0)
-
-    def beside(i, carry):
-        gsend[0, part(i), :] = normed_piece(flip(h, 1), i).astype(BF16)
-        gn_sib(0, i).start()
-        own_s[part(i), :] = normed_piece(h, i)
-        return carry
-
-    lax.fori_loop(0, pieces, beside, 0)
-
-    pg_sib[0].wait_recv()
-    pg_cross.wait_recv()
-    done = unpack(pg[0].astype(F32) + pgr[0].astype(F32) + pgr[2].astype(F32))
-    comb[:, 3 * cols :] = jnp.concatenate(done, axis=1).astype(BF16)
+    for j in range(pairs):
+        send_px(j).wait_recv()
+        pga[j] = (pgall[dp_rows(2 * j + side), :].astype(F32) + pgx[j].astype(F32)).astype(BF16)
+    for r in pair_order:
+        send_pz(r).start()
+
     load_gath.wait()
     for c in range(3):
         comb[:, c * cols : (c + 1) * cols] = dot(gradst[c * cols : (c + 1) * cols, :], gath[...]).T.astype(BF16)
     ones = jnp.ones((8, group), BF16)
     qb[...] = jnp.concatenate([dot(ones, grads[:, :cols])[:1], dot(ones, grads[:, 2 * cols :])[:1]], axis=1)
 
-    pairs = n_dp // 2
-    side, place = lax.rem(d, 2), lax.div(d, 2)
-
-    def comb_rows(index):
-        return pl.ds(pl.multiple_of(index * share, share), share)
-
     def send_side(j):
-        return remote(comb.at[comb_rows(2 * j + 1 - side), :], combx.at[j], qx_s.at[j], qx_r.at[j], at_dp(1))
+        return remote(comb.at[dp_rows(2 * j + 1 - side), :], combx.at[j], qx_s.at[j], qx_r.at[j], at_dp(1))
 
     def send_qg(r):
         return remote(comba.at[flip(place, r)], combr.at[r], qg_s.at[r], qg_r.at[r], at_dp(2 * r))
@@ -1013,28 +1037,31 @@
     def send_qb(r):
         return remote(qb, qbr.at[r], qb_s.at[r], qb_r.at[r], at_dp(r))
 
-    pair_order = list(range(pairs // 2, pairs)) + list(range(1, pairs // 2))
     for j in range(pairs):
         send_side(j).start()
     for r in order:
         send_qb(r).start()
-    for copy in sm_head:
-        copy.wait_recv()
-    total = sm_ref[...] + smr[1] + smr[2] + smr[3]
-    for e in range(n_dp):
-        smt[e] = (pltpu.roll(total, width - e * share, 1) if e else total)[:, :128]
-
-    def send_sm(r):
-        return remote(smt.at[flip(d, r)], smd.at[r], sd_s.at[r], sd_r.at[r], at_dp(r))
-
-    for r in order:
-        send_sm(r).start()
+    def beside(i, carry):
+        gsend[0, part(i), :] = normed_piece(flip(h, 1), i).astype(BF16)
+        gn_sib(0, i).start()
+        own_s[part(i), :] = normed_piece(h, i)
+        return carry
+
+    lax.fori_loop(0, pieces, beside, 0)
+
     for j in range(pairs):
         send_side(j).wait_recv()
-        comba[j] = (comb[comb_rows(2 * j + side), :].astype(F32) + combx[j].astype(F32)).astype(BF16)
+        comba[j] = (comb[dp_rows(2 * j + side), :].astype(F32) + combx[j].astype(F32)).astype(BF16)
     for r in pair_order:
         send_qg(r).start()
-
+    for r in order:
+        send_sm(r).wait_recv()
+    total = smt[d]
+    for r in range(1, n_dp):
+        total += smd[r]
+    smh[...] = total
+    for copy in sm_head:
+        copy.start()
     hot, flat_row, slot_row = slot_layouts(routes_ref[...], n_dp, cap)
     expert_row = jnp.sum(hot * lax.broadcasted_iota(jnp.int32, hot.shape, 0).astype(F32), axis=0, keepdims=True)
     flat_x = jnp.bitwise_xor(expert_row.astype(jnp.int32), d) * cap + slot_row
@@ -1071,7 +1098,15 @@
     en_head = [remote(en, enr.at[k], eh_s.at[k], eh_r.at[k], at_head(k)) for k in (1, 2, 3)]
     for copy in en_head:
         copy.start()
-    up_cross[1].start()
+    for r in pair_order:
+        send_pz(r).wait_recv()
+    total = pgall[dp_rows(d), :].astype(F32) + pgx[place].astype(F32)
+    for r in range(1, pairs):
+        total += pgz[r].astype(F32)
+    for b in range(4):
+        pgh[b] = total[:, b * cols : (b + 1) * cols].astype(BF16)
+    for k in (2, 3, 1):
+        send_ph(k).start()
     for copy in en_head:
         copy.wait_recv()
     ent[...] = en[...] + enr[1] + enr[2] + enr[3]
@@ -1083,19 +1118,22 @@
         send_qg(r).wait_recv()
     for r in order:
         send_qb(r).wait_recv()
-        send_sm(r).wait_recv()
-    total = comb[comb_rows(d), :].astype(F32) + combx[place].astype(F32)
+    total = comb[dp_rows(d), :].astype(F32) + combx[place].astype(F32)
     for r in range(1, pairs):
         total += combr[r].astype(F32)
-    comb_o[...] = total
+    comb_o[:, : 3 * cols] = total
+    total = pgh[h].astype(F32)
+    for k in (1, 2, 3):
+        send_ph(k).wait_recv()
+        total += pghr[k].astype(F32)
+    comb_o[:, 3 * cols :] = total
     sums = qb[...]
     for r in range(1, n_dp):
         sums += qbr[r]
     qb_o[...] = sums
-    total = smt[d]
-    for r in range(1, n_dp):
-        total += smd[r]
-    sums_o[...] = total
+    for copy in sm_head:
+        copy.wait_recv()
+    sums_o[...] = smh[...] + smr[1] + smr[2] + smr[3]
     for copy in bg_head:
         copy.wait_recv()
     bgs_o[...] = bg_ref[h] + bgr[1] + bgr[2] + bgr[3]
@@ -1118,8 +1156,13 @@
         send_side(j).wait_send()
     for copy in up_cross:
         copy.wait()
-    pg_cross.wait_send()
-    for copy in pg_sib + [gn_cross(i) for i in range(pieces)] + [gn_sib(j, i) for j in range(2) for i in range(pieces)] + sm_head + bg_head + en_head + en_dp:
+    for k in (1, 2, 3):
+        send_ph(k).wait_send()
+    for r in pair_order:
+        send_pz(r).wait_send()
+    for j in range(pairs):
+        send_px(j).wait_send()
+    for copy in [gn_cross(i) for i in range(pieces)] + [gn_sib(j, i) for j in range(2) for i in range(pieces)] + sm_head + bg_head + en_head + en_dp:
         copy.wait_send()
 
 
@@ -1131,7 +1174,6 @@
     share = width // n_dp
     sds = jax.ShapeDtypeStruct
     vm = pltpu.VMEM
-    packed = width * 3 // 2
     return pl.pallas_call(
         functools.partial(kernel_b, n_dp),
         out_shape=(
@@ -1144,24 +1186,27 @@
             sds((2, width), F32),
             sds(bg.shape[1:], F32),
         ),
-        in_specs=[VM, ANY, ANY, VM, VM, ANY] + [VM] * 8 + [ANY, ANY, VM, VM],
+        in_specs=[VM, ANY, ANY, VM, VM, ANY, ANY, ANY, VM, VM, VM, ANY, VM, VM, ANY, ANY, VM, VM],
         out_specs=(VM, VM, ANY) + (VM,) * 5,
         scratch_shapes=[
+            vm((3, cols, width), BF16), vm((tok, width), BF16), vm((tok, width), F32),
             vm(gctx.shape, BF16), vm((3, heads, group, hd), BF16), vm((group // TILE, heads, TILE, span), BF16), vm((group, width), BF16),
             vm(prod.shape, BF16),
             vm((heads, TILE, hd), BF16), vm((heads, hd, TILE), BF16), vm((heads, hd, TILE), BF16), vm((heads, TILE, 1), F32),
             vm((heads, TILE, hd), F32), vm((tok, width), F32), vm((tok, 1), jnp.int32), vm((cols, group), F32), vm((cols, group), F32), vm((group, 3 * cols), BF16), vm((3 * cols, group), BF16),
             vm((2, tok, width), BF16), vm((tok, width), BF16), vm((3, tok, width), BF16),
-            vm((width, 4 * cols), BF16), vm((n_dp // 2, share, 4 * cols), BF16), vm((n_dp // 2, share, 4 * cols), BF16),
-            vm((n_dp // 2, share, 4 * cols), BF16),
-            vm((4, packed, 128), BF16), vm((3, packed, 128), BF16), vm((width, tok), BF16),
+            vm((width, 3 * cols), BF16), vm((n_dp // 2, share, 3 * cols), BF16), vm((n_dp // 2, share, 3 * cols), BF16),
+            vm((n_dp // 2, share, 3 * cols), BF16),
+            vm((tok, width), BF16), vm((width, width), BF16), vm((n_dp // 2, share, width), BF16), vm((n_dp // 2, share, width), BF16),
+            vm((n_dp // 2, share, width), BF16), vm((4, share, cols), BF16), vm((4, share, cols), BF16), vm((width, tok), BF16),
             vm((1, 2 * cols), F32), vm((n_dp, 1, 2 * cols), F32),
-            vm((4,) + sm.shape, F32), vm((n_dp, sm.shape[0], 128), F32), vm((n_dp, sm.shape[0], 128), F32),
+            vm((4, sm.shape[0], 128), F32), vm((n_dp, sm.shape[0], 128), F32), vm((n_dp, sm.shape[0], 128), F32),
+            vm((sm.shape[0], 128), F32),
             vm((2, width), F32), vm((4, 2, width), F32), vm((2, width), F32), vm((n_dp, 2, width), F32),
             vm((4,) + bg.shape[1:], F32),
-            DMA((2,)), DMA((group // TILE,)), DMA((4,)), DMA((4,)), DMA((n_dp,)), DMA((n_dp,)), DMA((2,)), DMA((2,)), DMA((2, 2)), DMA((2, 2)),
-            DMA((2,)), DMA((2,)), DMA((n_dp // 2,)), DMA((n_dp // 2,)), DMA((n_dp // 2,)), DMA((n_dp // 2,)), DMA((3,)), DMA((3,)),
-            DMA((n_dp,)), DMA((n_dp,)),
+            DMA((5,)), DMA((group // TILE,)), DMA((4,)), DMA((4,)), DMA((n_dp,)), DMA((n_dp,)), DMA((2,)), DMA((2,)), DMA((2, 2)), DMA((2, 2)),
+            DMA((2,)), DMA((2,)), DMA((n_dp // 2,)), DMA((n_dp // 2,)), DMA((n_dp // 2,)), DMA((n_dp // 2,)),
+            DMA((n_dp // 2,)), DMA((n_dp // 2,)), DMA((n_dp // 2,)), DMA((n_dp // 2,)), DMA((4,)), DMA((4,)), DMA((n_dp,)), DMA((n_dp,)),
             DMA((4,)), DMA((4,)), DMA((n_dp,)), DMA((n_dp,)), DMA((4,)), DMA((4,)), DMA((n_dp,)), DMA((n_dp,)), DMA((4,)), DMA((4,)),
         ],
         compiler_params=pltpu.CompilerParams(collective_id=2, has_side_effects=True, vmem_limit_bytes=VMEM_LIMIT),

time: 232 us -> 221 us (0.953)
  Pallas kernels: 231 us -> 220 us
    pallas_call x1, Pallas kernels: 83.1 us -> 73.5 us  [stage_b(): pl.pallas_call(functools.partial(kernel_b, n_dp), out_shape=(sds((tok, wi...]
where the time goes in v1:
time: 221 us
  Pallas kernels  220 us (100%)
    pallas_call x1, Pallas kernels, stage_m(): pl.pallas_call(functools.partial(kernel_m, n_dp), out_shape=(sds((tok, wi...  84.7 us
    pallas_call x1, Pallas kernels, stage_b(): pl.pallas_call(functools.partial(kernel_b, n_dp), out_shape=(sds((tok, wi...  73.5 us
    pallas_call x1, Pallas kernels, stage_a(): pl.pallas_call(functools.partial(kernel_a, n_dp), out_shape=(sds((group,...  54.1 us
    pallas_call x1, Pallas kernels, stage_f(): pl.pallas_call(functools.partial(kernel_f, n_dp), out_shape=outs, grid=(s...  7.52 us

profile of v1, /device:TPU:0, one launch (start us, length us, event | category | flops | bytes accessed | tf_op | source)
XLA Modules:
  0.0 220.6 jit_solution(15238551455597601260)
XLA Ops:
  0.6 54.1 %shard_map.288 = (bf16[2048,768]{1,0:T(8,128)(2,1)}, bf16[3,3,2048,64]{3,2,1,0:T(8,128)(2,1)}, bf16[3,8,256,1280]{3,2,1,0:T(8,128)(2,1)}, bf16[8,384,128]{2,1,0:...) custom-call(bf16[512,768]{1,0:T(8,128)(2,1)} %x_h.1, ...), custom_call_target="tpu_custom_call" | custom-call | tf_op jit(solution)/shard_map/pallas_call | solution.py:315
  54.8 84.7 %shard_map.289 = (f32[512,768]{1,0:T(8,128)}, f32[512,1]{1,0:T(8,128)}, bf16[1024,768]{1,0:T(8,128)(2,1)}, f32[512,768]{1,0:T(8,128)}, bf16[4,768,128]{2,1,0:T(8...) custom-call(bf16[512,768]{1,0:T(8,128)(2,1)} %x_h.1, ...), custom_call_target="tpu_custom_call" | custom-call | tf_op jit(solution)/shard_map/pallas_call | solution.py:717
  139.4 73.5 %shard_map.290 = (bf16[512,768]{1,0:T(8,128)(2,1)}, f32[512,768]{1,0:T(8,128)}, bf16[768,768]{1,0:T(8,128)(2,1)}, f32[96,768]{1,0:T(8,128)}, f32[1,384]{1,0:T(1,...) custom-call(bf16[4,768,128]{2,1,0:T(8,128)(2,1)} %get-tuple-element.62.gctx, ...), custom_call_target="tpu_custom_call" | custom-call | tf_op jit(solution)/shard_map/pallas_call | solution.py:1177
  212.9 7.5 %shard_map.291 = (bf16[512,768]{1,0:T(8,128)(2,1)}, f32[1]{0:T(128)}, f32[512,768]{1,0:T(8,128)}, f32[24]{0:T(128)}, f32[24]{0:T(128)}, /*index=5*/f32[3,96,192]...) custom-call(bf16[512,768]{1,0:T(8,128)(2,1)} %get-tuple-element.74.m, ...), custom_call_target="tpu_custom_call" | custom-call | tf_op jit(solution)/shard_map/pallas_call | solution.py:1279

commit v2 on v1

--- a/solution.py
+++ b/solution.py
@@ -246,7 +246,7 @@
 
     before = 0
     for t in range(low_tiles):
-        tile_step(t, (t + 1) * TILE, before, False)
+        tile_step(t, (t + 1) * TILE, before, t >= 3)
         before = (t + 1) * TILE
     span = reach * TILE
     p_st[:, :, before:] = jnp.zeros((heads, TILE, span - before), BF16)
@@ -961,7 +961,7 @@
         @pl.when(turn == 0)
         def _():
             for t in range(half):
-                attention(t, (t + 1) * TILE, False)
+                attention(t, (t + 1) * TILE, t >= 2)
 
         @pl.when(turn == 1)
         def _():

time: 221 us -> 219 us (level)
  no operation moved by 1% of the time
where the time goes in v2:
time: 219 us
  Pallas kernels  218 us (100%)
    pallas_call x1, Pallas kernels, stage_m(): pl.pallas_call(functools.partial(kernel_m, n_dp), out_shape=(sds((tok, wi...  84.3 us
    pallas_call x1, Pallas kernels, stage_b(): pl.pallas_call(functools.partial(kernel_b, n_dp), out_shape=(sds((tok, wi...  72.5 us
    pallas_call x1, Pallas kernels, stage_a(): pl.pallas_call(functools.partial(kernel_a, n_dp), out_shape=(sds((group,...  53.7 us
    pallas_call x1, Pallas kernels, stage_f(): pl.pallas_call(functools.partial(kernel_f, n_dp), out_shape=outs, grid=(s...  7.52 us

profile of v2, /device:TPU:0, one launch (start us, length us, event | category | flops | bytes accessed | tf_op | source)
XLA Modules:
  0.0 218.9 jit_solution(6715792518790052744)
XLA Ops:
  0.6 53.7 %shard_map.288 = (bf16[2048,768]{1,0:T(8,128)(2,1)}, bf16[3,3,2048,64]{3,2,1,0:T(8,128)(2,1)}, bf16[3,8,256,1280]{3,2,1,0:T(8,128)(2,1)}, bf16[8,384,128]{2,1,0:...) custom-call(bf16[512,768]{1,0:T(8,128)(2,1)} %x_h.1, ...), custom_call_target="tpu_custom_call" | custom-call | tf_op jit(solution)/shard_map/pallas_call | solution.py:315
  54.4 84.3 %shard_map.289 = (f32[512,768]{1,0:T(8,128)}, f32[512,1]{1,0:T(8,128)}, bf16[1024,768]{1,0:T(8,128)(2,1)}, f32[512,768]{1,0:T(8,128)}, bf16[4,768,128]{2,1,0:T(8...) custom-call(bf16[512,768]{1,0:T(8,128)(2,1)} %x_h.1, ...), custom_call_target="tpu_custom_call" | custom-call | tf_op jit(solution)/shard_map/pallas_call | solution.py:717
  138.7 72.5 %shard_map.290 = (bf16[512,768]{1,0:T(8,128)(2,1)}, f32[512,768]{1,0:T(8,128)}, bf16[768,768]{1,0:T(8,128)(2,1)}, f32[96,768]{1,0:T(8,128)}, f32[1,384]{1,0:T(1,...) custom-call(bf16[4,768,128]{2,1,0:T(8,128)(2,1)} %get-tuple-element.62.gctx, ...), custom_call_target="tpu_custom_call" | custom-call | tf_op jit(solution)/shard_map/pallas_call | solution.py:1177
  211.2 7.5 %shard_map.291 = (bf16[512,768]{1,0:T(8,128)(2,1)}, f32[1]{0:T(128)}, f32[512,768]{1,0:T(8,128)}, f32[24]{0:T(128)}, f32[24]{0:T(128)}, /*index=5*/f32[3,96,192]...) custom-call(bf16[512,768]{1,0:T(8,128)(2,1)} %get-tuple-element.74.m, ...), custom_call_target="tpu_custom_call" | custom-call | tf_op jit(solution)/shard_map/pallas_call | solution.py:1279
